TPU v7x, 512 devices: a whole 4x4x16 slice. The times are simulated.
512 devices in a mesh: sec: 8 (over x, core), xy: 64 (over y, z).
Axes of the slice: x: 4, y: 4, z: 16, core: 2. Of those that a mesh axis runs over, the one named last changes fastest.
Arguments:
- source: bfloat16 [8, 32768, 1024], P('sec', 'xy'), may hold values from -6 to 6
- coarse: int32 [8, 2, 128], P('sec', None, 'xy'), may hold values from -1 to 1, as said below
- fraction: float32 [8, 2, 128], P('sec', None, 'xy'), may hold values from 0.25 to 0.75
- kernel_one: float32 [3, 3, 3], replicated, may hold values from -1.25 to 1.25
- kernel_two: float32 [3, 3, 3], replicated, may hold values from -1.25 to 1.25
Outputs:
- denoised: bfloat16 [8, 1024, 32768], P(None, 'xy', 'sec')
Inputs may be any that keep to these rules, and one draw needn't show every extreme that they name: Destination block (r, c) reads source block (r + coarse[z, 0, b], c + coarse[z, 1, b]); c + coarse[z, 1, b] always lies in 0 to 1. Among the 2 blocks of one block row of a section, at most one has a row offset of -1 and at most one has +1.
All inputs are finite; a program needn't handle non-finite values.
Results may differ from a plain program's by a relative error of at most 0.003.
The roundings to bfloat16 on the way count: a program that leaves them out, or rounds other values in their place, can miss the bound.
Values may be sent and summed in bfloat16 or wider, within the bound.
No kernel may reach another device: no remote copies, remote signals or barrier semaphores. Data moves between devices by JAX's collectives and lax.ppermute only.
A program may use at most 128 MiB of HBM per device.

v0:
```python
import jax
import jax.numpy as jnp
from jax import lax
from jax.sharding import PartitionSpec as P


def from_behind(value, axis, steps):
    count = lax.axis_size(axis)
    first, last = (max(0, -steps), min(count, count - steps))
    return lax.ppermute(value, axis, [(source, source + steps) for source in range(first, last)])


def with_halo(x, sides, width):
    for axis, dim in sides:
        size, length = (lax.axis_size(axis), x.shape[dim])
        up = [(i, (i + 1) % size) for i in range(size - 1)]
        down = [(j, i) for i, j in up]
        last = lax.slice_in_dim(x, length - width, length, axis=dim)
        first = lax.slice_in_dim(x, 0, width, axis=dim)
        before = lax.ppermute(last, axis, up)
        after = lax.ppermute(first, axis, down)
        x = jnp.concatenate([before, x, after], axis=dim)
    return x


def interpolation(shift, edge):
    row_index = lax.broadcasted_iota(jnp.int32, (edge, edge), 0)
    col_index = lax.broadcasted_iota(jnp.int32, (edge, edge), 1)
    offset = col_index - row_index
    amount = shift[..., None, None]
    w_before = ((-0.5 * amount + 1.0) * amount - 0.5) * amount
    w_center = (1.5 * amount - 2.5) * amount * amount + 1.0
    w_after = ((-1.5 * amount + 2.0) * amount + 0.5) * amount
    w_beyond = (0.5 * amount - 0.5) * amount * amount
    matrix = jnp.where(offset == -1, w_before, 0.0) + jnp.where(offset == 0, w_center, 0.0)
    matrix = matrix + jnp.where(offset == 1, w_after, 0.0) + jnp.where(offset == 2, w_beyond, 0.0)
    return matrix.astype(jnp.bfloat16)


def pad_sections(volume):
    return jnp.pad(volume, ((1, 1), (0, 0), (0, 0)))


def stencil(padded, kernel, depth, cols_out, rows_out):
    running = jnp.zeros((depth, cols_out, rows_out), jnp.float32)
    for tap_z in range(3):
        for tap_x in range(3):
            for tap_y in range(3):
                window = padded[
                    tap_z : tap_z + depth, tap_x : tap_x + cols_out, tap_y : tap_y + rows_out
                ]
                running = running + kernel[tap_z, tap_x, tap_y] * window
    return running


def body(source, coarse, fraction, kernel_one, kernel_two):
    sections_dev, edge, width = source.shape
    columns = width // edge
    row_shift = coarse[:, 0, :]
    col_shift = coarse[:, 1, :]
    target = lax.broadcasted_iota(jnp.int32, (sections_dev, columns, columns), 1)
    anchor = lax.broadcasted_iota(jnp.int32, (sections_dev, columns, columns), 2)
    from_above = from_behind(source, "xy", 1)
    from_below = from_behind(source, "xy", -1)
    stacked = jnp.stack([from_above, source, from_below]).reshape(
        3, sections_dev, edge, columns, edge
    )
    level = lax.broadcasted_iota(jnp.int32, (3, sections_dev, columns, columns), 0)
    choose = (row_shift[None, :, :, None] + 1 == level) & (
        target[None] + col_shift[None, :, :, None] == anchor[None]
    )
    picked = jnp.einsum(
        "ksnm,ksimj->snij", choose.astype(jnp.bfloat16), stacked, preferred_element_type=jnp.float32
    ).astype(jnp.bfloat16)
    row_matrix = interpolation(fraction[:, 0, :], edge)
    col_matrix = interpolation(fraction[:, 1, :], edge)
    rows_warped = jnp.einsum(
        "snij,snjk->snik", row_matrix, picked, preferred_element_type=jnp.float32
    ).astype(jnp.bfloat16)
    warped = jnp.einsum(
        "sncj,snrj->sncr", col_matrix, rows_warped, preferred_element_type=jnp.float32
    ).astype(jnp.bfloat16)
    aligned_strip = warped.reshape(sections_dev, width, edge)
    group_data = lax.all_to_all(
        lax.all_to_all(aligned_strip, "xy", split_axis=1, concat_axis=2, tiled=True),
        "sec",
        split_axis=2,
        concat_axis=0,
        tiled=True,
    )
    sections_all, group_cols, group_rows = group_data.shape
    rim_one = with_halo(group_data, (("sec", 2), ("xy", 1)), 1)
    first_pass = jnp.maximum(
        stencil(
            pad_sections(rim_one.astype(jnp.float32)),
            kernel_one,
            sections_all,
            group_cols,
            group_rows,
        ),
        0.0,
    ).astype(jnp.bfloat16)
    rim_two = with_halo(first_pass, (("sec", 2), ("xy", 1)), 1)
    second = stencil(
        pad_sections(rim_two.astype(jnp.float32)), kernel_two, sections_all, group_cols, group_rows
    )
    return (second + group_data.astype(jnp.float32)).astype(jnp.bfloat16)


def solution(mesh):
    placed = (P("sec", "xy", None), P("sec", None, "xy"), P("sec", None, "xy"), P(), P())
    return jax.shard_map(
        body, mesh=mesh, in_specs=placed, out_specs=P(None, "xy", "sec"), check_vma=False
    )
```

profile of v0, /device:TPU:9, one launch (start us, length us, event | category | flops | bytes accessed | tf_op | source)
XLA Modules:
  0.0 503.7 jit_solution(17445958585612541648)
XLA Ops:
  0.0 3.7 collective-permute-start
  3.7 9.4 %collective-permute-start.1 = (bf16[1,512,1024]{2,1,0:T(8,128)(2,1)}, bf16[1,512,1024]{2,1,0:T(8,128)(2,1)S(1)}, u32[]{:S(2)}, u32[]{:S(2)}) collective-permute-start(bf16[1,512,1024]{2,1,0:T(8,128)(2,1)} %param.5), channel_id=1, source_target_pairs={{1,0},{2,1},{3,2},{4,3},{5,4},{6,5},{7,6},{8,7},{9,8},{10,9},{11,1... | collective-permute-start | bytes 3145736 | tf_op jit(solution)/shard_map/ppermute | solution.py:10
  16.9 17.3 %collective-permute-done = bf16[1,512,1024]{2,1,0:T(8,128)(2,1)S(1)} collective-permute-done((bf16[1,512,1024]{2,1,0:T(8,128)(2,1)}, bf16[1,512,1024]{2,1,0:T(8,128)(2,1)S(1)}, u32[]{:S(2)}, u32[]{:S(2)}) %collective-permute-start) | collective-permute-done | bytes 1048608 | tf_op jit(solution)/shard_map/ppermute | solution.py:10
  36.6 8.0 %bitcast_convert_fusion = bf16[2,512,512]{2,0,1:T(2,128)(2,1)} fusion(bf16[1,1,512,2,512]{4,3,0,2,1:T(2,128)(2,1)S(1)} %stack.14, bf16[1,1,512,2,512]{4,3,0,2,1:T(2,128)(2,1)S(1)} %stack.13, bf16[1,1,512,2,512]{4,3,0,2,1:T(2,128)(2,1)} %stack.12, pred[3,2,2]{2,0,1:T(4,128)(4,1)S(1)} %fusion.122), kind=kOutput, calls=%fused_computation.148 | convolution fusion | flops 16252928 | bytes 4194316 | tf_op jit(solution)/shard_map/ksnm,ksimj->snij/dot_general | solution.py:72
  44.6 3.9 convolution_convert_fusion
  50.7 7.0 %reduce = bf16[1024,512]{1,0:T(8,128)(2,1)S(1)} reduce(bf16[1024,1,512]{2,1,0:T(2,128)(2,1)S(1)} %bitcast.173, bf16[]{:T(256)} %broadcast.323), dimensions={1}, to_apply=%bitcast.165.reduce_sub_computation | reduce | bytes 2097154
  58.5 60.3 %all_to_all.36 = bf16[64,2,4096]{2,1,0:T(2,128)(2,1)S(1)} all-to-all(bf16[64,2,4096]{2,1,0:T(2,128)(2,1)S(1)} %reshape.317), channel_id=1, replica_groups=mesh['sec'=8,'xy'=64] {'xy'}, dimensions={0} | all-to-all | bytes 2097152 | tf_op jit(solution)/shard_map/all_to_all | solution.py:85
  120.2 25.0 %copy.15 = bf16[1,16,32768]{1,0,2:T(2,128)(2,1)} copy(bf16[1,16,32768]{2,1,0:T(8,128)(2,1)S(1)} %bitcast.175) | data formatting | bytes 2097152 | tf_op jit(solution)/shard_map/all_to_all | solution.py:85
  145.2 179.2 %reduce.1 = bf16[32768,16]{1,0:T(8,128)(2,1)} reduce(bf16[32768,1,16]{2,1,0:T(2,128)(2,1)} %bitcast.168, bf16[]{:T(256)} %broadcast.323), dimensions={1}, to_apply=%bitcast.162.reduce_sub_computation | reduce | bytes 2097154
  324.4 10.4 %reshape.319 = bf16[8,2,32768]{2,1,0:T(2,128)(2,1)S(1)} reshape(bf16[32768,16]{1,0:T(8,128)(2,1)} %reduce.1) | data formatting | bytes 2097152
  334.8 25.2 %all_to_all.37 = bf16[8,2,32768]{2,1,0:T(2,128)(2,1)S(1)} all-to-all(bf16[8,2,32768]{2,1,0:T(2,128)(2,1)S(1)} %reshape.319), channel_id=1, replica_groups=mesh['sec'=8,'xy'=64] {'sec'}, dimensions={0} | all-to-all | bytes 2097152 | tf_op jit(solution)/shard_map/all_to_all | solution.py:84
  360.0 12.2 %reshape.320 = bf16[32768,1,16]{2,1,0:T(2,128)(2,1)} reshape(bf16[8,2,32768]{2,1,0:T(2,128)(2,1)S(1)} %all_to_all.37) | data formatting | bytes 2097152
  372.3 29.6 %copy.16 = bf16[1,16,32768]{2,1,0:T(8,128)(2,1)S(1)} copy(bf16[1,16,32768]{1,0,2:T(2,128)(2,1)} %bitcast.169) | data formatting | bytes 2097152 | tf_op jit(solution)/shard_map/all_to_all | solution.py:84
  402.7 3.1 collective-permute-start.2
  408.5 2.6 collective-permute-done.3
  412.7 3.1 collective-permute-start.4
  415.8 4.6 collective-permute-start.5
  422.9 27.6 %fusion.43 = bf16[8,16,4096]{2,0,1:T(8,128)(2,1)} fusion(f32[8,18,4098]{2,0,1:T(8,128)S(1)} %maximum_convert_fusion, f32[]{:T(128)} %bitcast.41, f32[]{:T(128)} %bitcast.40, f32[]{:T(128)} %bitcast.39, f32[]{:T(128)} %bitcast.38, f32[]{:T(128)} %bitcast.37, f32[]{:T(128)} %bitcast.36, f32[]{:T(128)} %bitcast.35, f32[]{:T(128)} %bitcast.34, f32[]{:T(128)} %bitcast.33, ...), kind=kLoop, calls=%fused_computation.80 | loop fusion | flops 28835840 | bytes 22356076 | tf_op jit(solution)/shard_map/convert_element_type | solution.py:102
  451.3 3.0 collective-permute-start.6
  457.0 2.6 collective-permute-done.7
  459.6 2.9 concatenate.15
  464.8 5.7 %collective-permute-start.9 = (bf16[8,1,4098]{2,0,1:T(8,128)(2,1)S(1)}, bf16[8,1,4098]{2,0,1:T(8,128)(2,1)S(1)}, u32[]{:S(2)}, u32[]{:S(2)}) collective-permute-start(bf16[8,1,4098]{2,0,1:T(8,128)(2,1)S(1)} %get-tuple-element.6), channel_id=1, source_target_pairs={{1,0},{2,1},{3,2},{4,3},{5,4},{6,5},{7,6},{8,7},{9,8},{10,9},{11,1... | collective-permute-start | bytes 196712 | tf_op jit(solution)/shard_map/ppermute | solution.py:21
  473.3 27.6 %fusion.89 = bf16[8,16,4096]{2,0,1:T(8,128)(2,1)} fusion(f32[8,18,4098]{2,0,1:T(8,128)S(1)} %maximum_convert_fusion.1, f32[]{:T(128)} %bitcast.67, f32[]{:T(128)} %bitcast.66, f32[]{:T(128)} %bitcast.65, f32[]{:T(128)} %bitcast.64, f32[]{:T(128)} %bitcast.63, f32[]{:T(128)} %bitcast.62, f32[]{:T(128)} %bitcast.61, f32[]{:T(128)} %bitcast.60, f32[]{:T(128)} %bitcast.59, ...), kind=kLoop, calls=%fused_computation.126 | loop fusion | flops 29360128 | bytes 23404652 | tf_op jit(solution)/shard_map/convert_element_type | solution.py:107
  500.9 2.8 copy.17
  (56 shorter events, 26.6 us)
Async XLA Ops:
  0.0 16.8 %copy-start.8 = (s32[1,2,2]{2,1,0:T(2,128)S(1)}, s32[1,2,2]{2,1,0:T(2,128)}, u32[]{:S(2)}) copy-start(s32[1,2,2]{2,1,0:T(2,128)} %param.6) | copy-start | bytes 52
  0.0 16.9 %copy-start.7 = (f32[1,2,2]{2,1,0:T(2,128)S(1)}, f32[1,2,2]{2,1,0:T(2,128)}, u32[]{:S(2)}) copy-start(f32[1,2,2]{2,1,0:T(2,128)} %param.7) | copy-start | bytes 52
  0.0 34.2 %collective-permute-start = (bf16[1,512,1024]{2,1,0:T(8,128)(2,1)}, bf16[1,512,1024]{2,1,0:T(8,128)(2,1)S(1)}, u32[]{:S(2)}, u32[]{:S(2)}) collective-permute-start(bf16[1,512,1024]{2,1,0:T(8,128)(2,1)} %param.5), channel_id=1, source_target_pairs={{0,1},{1,2},{2,3},{3,4},{4,5},{5,6},{6,7},{7,8},{8,9},{9,10},{10,1... | collective-permute-start | bytes 3145736 | tf_op jit(solution)/shard_map/ppermute | solution.py:10
  3.7 32.1 %collective-permute-start.1 = (bf16[1,512,1024]{2,1,0:T(8,128)(2,1)}, bf16[1,512,1024]{2,1,0:T(8,128)(2,1)S(1)}, u32[]{:S(2)}, u32[]{:S(2)}) collective-permute-start(bf16[1,512,1024]{2,1,0:T(8,128)(2,1)} %param.5), channel_id=1, source_target_pairs={{1,0},{2,1},{3,2},{4,3},{5,4},{6,5},{7,6},{8,7},{9,8},{10,9},{11,1... | collective-permute-start | bytes 3145736 | tf_op jit(solution)/shard_map/ppermute | solution.py:10
  36.6 8.0 %copy-start.2 = (pred[512,512]{1,0:T(8,128)(4,1)S(1)}, pred[512,512]{1,0:T(8,128)(4,1)}, u32[]{:S(2)}) copy-start(pred[512,512]{1,0:T(8,128)(4,1)} %get-tuple-element.78) | copy-start | bytes 786436
  36.6 8.0 %copy-start.3 = (pred[512,512]{1,0:T(8,128)(4,1)S(1)}, pred[512,512]{1,0:T(8,128)(4,1)}, u32[]{:S(2)}) copy-start(pred[512,512]{1,0:T(8,128)(4,1)} %get-tuple-element.79) | copy-start | bytes 786436
  36.6 8.0 %copy-start.4 = (pred[512,512]{1,0:T(8,128)(4,1)S(1)}, pred[512,512]{1,0:T(8,128)(4,1)}, u32[]{:S(2)}) copy-start(pred[512,512]{1,0:T(8,128)(4,1)} %get-tuple-element.80) | copy-start | bytes 786436
  401.9 5.8 %copy-start.5 = (f32[3,3,3]{2,1,0:T(4,128)S(1)}, f32[3,3,3]{2,1,0:T(4,128)}, u32[]{:S(2)}) copy-start(f32[3,3,3]{2,1,0:T(4,128)} %param.8) | copy-start | bytes 328
  402.7 5.8 %collective-permute-start.2 = (bf16[8,16,1]{2,0,1:T(8,128)(2,1)S(1)}, bf16[8,16,1]{2,0,1:T(8,128)(2,1)S(1)}, u32[]{:S(2)}, u32[]{:S(2)}) collective-permute-start(bf16[8,16,1]{2,0,1:T(8,128)(2,1)S(1)} %get-tuple-element.12), channel_id=1, source_target_pairs={{0,64},{64,128},{128,192},{192,256},{256,320},{320,384},{384,448},... | collective-permute-start | bytes 776 | tf_op jit(solution)/shard_map/ppermute | solution.py:20
  405.8 5.2 %collective-permute-start.3 = (bf16[8,16,1]{2,0,1:T(8,128)(2,1)S(1)}, bf16[8,16,1]{2,0,1:T(8,128)(2,1)S(1)}, u32[]{:S(2)}, u32[]{:S(2)}) collective-permute-start(bf16[8,16,1]{2,0,1:T(8,128)(2,1)S(1)} %get-tuple-element.11), channel_id=1, source_target_pairs={{64,0},{128,64},{192,128},{256,192},{320,256},{384,320},{448,384},... | collective-permute-start | bytes 776 | tf_op jit(solution)/shard_map/ppermute | solution.py:21
  412.7 8.4 %copy-start = (bf16[8,16,4098]{2,0,1:T(8,128)(2,1)}, bf16[8,16,4098]{2,0,1:T(8,128)(2,1)S(1)}, u32[]{:S(2)}) copy-start(bf16[8,16,4098]{2,0,1:T(8,128)(2,1)S(1)} %concatenate.13) | copy-start | bytes 3147268
  412.7 8.4 %collective-permute-start.4 = (bf16[8,1,4098]{2,0,1:T(8,128)(2,1)S(1)}, bf16[8,1,4098]{2,0,1:T(8,128)(2,1)S(1)}, u32[]{:S(2)}, u32[]{:S(2)}) collective-permute-start(bf16[8,1,4098]{2,0,1:T(8,128)(2,1)S(1)} %get-tuple-element.7), channel_id=1, source_target_pairs={{0,1},{1,2},{2,3},{3,4},{4,5},{5,6},{6,7},{7,8},{8,9},{9,10},{10,1... | collective-permute-start | bytes 196712 | tf_op jit(solution)/shard_map/ppermute | solution.py:20
  415.8 5.7 %collective-permute-start.5 = (bf16[8,1,4098]{2,0,1:T(8,128)(2,1)S(1)}, bf16[8,1,4098]{2,0,1:T(8,128)(2,1)S(1)}, u32[]{:S(2)}, u32[]{:S(2)}) collective-permute-start(bf16[8,1,4098]{2,0,1:T(8,128)(2,1)S(1)} %get-tuple-element.8), channel_id=1, source_target_pairs={{1,0},{2,1},{3,2},{4,3},{5,4},{6,5},{7,6},{8,7},{9,8},{10,9},{11,1... | collective-permute-start | bytes 196712 | tf_op jit(solution)/shard_map/ppermute | solution.py:21
  422.9 33.4 %copy-start.6 = (f32[3,3,3]{2,1,0:T(4,128)S(1)}, f32[3,3,3]{2,1,0:T(4,128)}, u32[]{:S(2)}) copy-start(f32[3,3,3]{2,1,0:T(4,128)} %param.9) | copy-start | bytes 328
  451.3 5.7 %collective-permute-start.6 = (bf16[8,16,1]{2,0,1:T(8,128)(2,1)S(1)}, bf16[8,16,1]{2,0,1:T(8,128)(2,1)S(1)}, u32[]{:S(2)}, u32[]{:S(2)}) collective-permute-start(bf16[8,16,1]{2,0,1:T(8,128)(2,1)S(1)} %get-tuple-element.10), channel_id=1, source_target_pairs={{0,64},{64,128},{128,192},{192,256},{256,320},{320,384},{384,448},... | collective-permute-start | bytes 776 | tf_op jit(solution)/shard_map/ppermute | solution.py:20
  454.3 5.2 %collective-permute-start.7 = (bf16[8,16,1]{2,0,1:T(8,128)(2,1)S(1)}, bf16[8,16,1]{2,0,1:T(8,128)(2,1)S(1)}, u32[]{:S(2)}, u32[]{:S(2)}) collective-permute-start(bf16[8,16,1]{2,0,1:T(8,128)(2,1)S(1)} %get-tuple-element.9), channel_id=1, source_target_pairs={{64,0},{128,64},{192,128},{256,192},{320,256},{384,320},{448,384},... | collective-permute-start | bytes 776 | tf_op jit(solution)/shard_map/ppermute | solution.py:21
  462.5 8.7 %copy-start.1 = (bf16[8,16,4098]{2,0,1:T(8,128)(2,1)}, bf16[8,16,4098]{2,0,1:T(8,128)(2,1)S(1)}, u32[]{:S(2)}) copy-start(bf16[8,16,4098]{2,0,1:T(8,128)(2,1)S(1)} %concatenate.15) | copy-start | bytes 3147268
  462.5 8.7 %collective-permute-start.8 = (bf16[8,1,4098]{2,0,1:T(8,128)(2,1)S(1)}, bf16[8,1,4098]{2,0,1:T(8,128)(2,1)S(1)}, u32[]{:S(2)}, u32[]{:S(2)}) collective-permute-start(bf16[8,1,4098]{2,0,1:T(8,128)(2,1)S(1)} %get-tuple-element.5), channel_id=1, source_target_pairs={{0,1},{1,2},{2,3},{3,4},{4,5},{5,6},{6,7},{7,8},{8,9},{9,10},{10,1... | collective-permute-start | bytes 196712 | tf_op jit(solution)/shard_map/ppermute | solution.py:20
  464.8 7.0 %collective-permute-start.9 = (bf16[8,1,4098]{2,0,1:T(8,128)(2,1)S(1)}, bf16[8,1,4098]{2,0,1:T(8,128)(2,1)S(1)}, u32[]{:S(2)}, u32[]{:S(2)}) collective-permute-start(bf16[8,1,4098]{2,0,1:T(8,128)(2,1)S(1)} %get-tuple-element.6), channel_id=1, source_target_pairs={{1,0},{2,1},{3,2},{4,3},{5,4},{6,5},{7,6},{8,7},{9,8},{10,9},{11,1... | collective-permute-start | bytes 196712 | tf_op jit(solution)/shard_map/ppermute | solution.py:21
where the time goes:
time: 506 us; the launch traced here: 504 us
  other arithmetic  246 us (49%)
  local copies, waits for them, and re-layouts  97.5 us (19%)
  blocking collectives  85.5 us (17%)
  starting transfers between devices  38.7 us (8%)
  waiting for transfers between devices  23.4 us (5%)
  matrix products  11.9 us (2%)
    unnamed x2, other arithmetic  186 us
    all_to_all x1, blocking collectives, body(): lax.all_to_all(aligned_strip, 'xy', split_axis=1, concat_axis=2, tiled=True)  60.3 us
    all_to_all x2, local copies, waits for them, and re-layouts, body(): lax.all_to_all(lax.all_to_all(aligned_strip, 'xy', split_axis=1, concat_a...  29.7 us
    convert_element_type x1, other arithmetic, body(): return (second + group_data.astype(jnp.float32)).astype(jnp.bfloat16)  27.6 us
    convert_element_type x1, other arithmetic, body(): first_pass = jnp.maximum(stencil(pad_sections(rim_one.astype(jnp.float32)...  27.6 us
    unnamed x25, local copies, waits for them, and re-layouts  25.9 us
    all_to_all x1, blocking collectives, body(): lax.all_to_all(lax.all_to_all(aligned_strip, 'xy', split_axis=1, concat_a...  25.2 us
    all_to_all x2, local copies, waits for them, and re-layouts, body(): lax.all_to_all(aligned_strip, 'xy', split_axis=1, concat_axis=2, tiled=True)  25.1 us
  transfers between devices with their start and end apart: 10, of which 5 were waited for; matrix products, arithmetic and copies ran while one was open for 2% of the time, Pallas kernels for 0%

commit v1 on v0

--- a/solution.py
+++ b/solution.py
@@ -81,12 +81,17 @@
         "sncj,snrj->sncr", col_matrix, rows_warped, preferred_element_type=jnp.float32
     ).astype(jnp.bfloat16)
     aligned_strip = warped.reshape(sections_dev, width, edge)
+    search_circles = lambda local_array: jnp.concatenate(
+        lax.all_to_all(
+            jnp.stack(jnp.split(local_array, lax.axis_size("xy"), axis=1)),
+            axis_name="xy",
+            split_axis=0,
+            concat_axis=0,
+        ),
+        2,
+    )
     group_data = lax.all_to_all(
-        lax.all_to_all(aligned_strip, "xy", split_axis=1, concat_axis=2, tiled=True),
-        "sec",
-        split_axis=2,
-        concat_axis=0,
-        tiled=True,
+        search_circles(aligned_strip), "sec", split_axis=2, concat_axis=0, tiled=True
     )
     sections_all, group_cols, group_rows = group_data.shape
     rim_one = with_halo(group_data, (("sec", 2), ("xy", 1)), 1)

time: 506 us -> 496 us (0.980)
  other arithmetic: 246 us -> 239 us
    all_to_all x4 -> x2, local copies, waits for them, and re-layouts: 54.8 us -> 29.7 us  [body(): lax.all_to_all(search_circles(aligned_strip), 'sec', split_axis=2, concat...]
    reshape x1 -> x2, local copies, waits for them, and re-layouts: 1.62 us -> 25.1 us  [body(): jnp.concatenate(lax.all_to_all(jnp.stack(jnp.split(local_array, lax.axis_...]
    unnamed x2 -> x1, other arithmetic: 186 us -> 179 us
    unnamed x25 -> x85, local copies, waits for them, and re-layouts: 25.9 us -> 24 us
where the time goes in v1:
time: 496 us; the launch traced here: 494 us
  other arithmetic  239 us (48%)
  local copies, waits for them, and re-layouts  94.1 us (19%)
  blocking collectives  85.5 us (17%)
  starting transfers between devices  38.7 us (8%)
  waiting for transfers between devices  23.5 us (5%)
  matrix products  11.9 us (2%)
    unnamed x1, other arithmetic  179 us
    all_to_all x1, blocking collectives, body(): lax.all_to_all(jnp.stack(jnp.split(local_array, lax.axis_size('xy'), axis...  60.3 us
    all_to_all x2, local copies, waits for them, and re-layouts, body(): lax.all_to_all(search_circles(aligned_strip), 'sec', split_axis=2, concat...  29.7 us
    convert_element_type x1, other arithmetic, body(): return (second + group_data.astype(jnp.float32)).astype(jnp.bfloat16)  27.7 us
    convert_element_type x1, other arithmetic, body(): first_pass = jnp.maximum(stencil(pad_sections(rim_one.astype(jnp.float32)...  27.6 us
    all_to_all x1, blocking collectives, body(): lax.all_to_all(search_circles(aligned_strip), 'sec', split_axis=2, concat...  25.3 us
    reshape x2, local copies, waits for them, and re-layouts, body(): jnp.concatenate(lax.all_to_all(jnp.stack(jnp.split(local_array, lax.axis_...  25.1 us
    unnamed x85, local copies, waits for them, and re-layouts  24 us
  transfers between devices with their start and end apart: 10, of which 5 were waited for; matrix products, arithmetic and copies ran while one was open for 2% of the time, Pallas kernels for 0%

profile of v1, /device:TPU:9, one launch (start us, length us, event | category | flops | bytes accessed | tf_op | source)
XLA Modules:
  0.0 493.9 jit_solution(16365179551710661039)
XLA Ops:
  0.0 3.7 collective-permute-start
  3.7 9.4 %collective-permute-start.1 = (bf16[1,512,1024]{2,1,0:T(8,128)(2,1)}, bf16[1,512,1024]{2,1,0:T(8,128)(2,1)S(1)}, u32[]{:S(2)}, u32[]{:S(2)}) collective-permute-start(bf16[1,512,1024]{2,1,0:T(8,128)(2,1)} %param.5), channel_id=1, source_target_pairs={{1,0},{2,1},{3,2},{4,3},{5,4},{6,5},{7,6},{8,7},{9,8},{10,9},{11,1... | collective-permute-start | bytes 3145736 | tf_op jit(solution)/shard_map/ppermute | solution.py:10
  17.0 17.3 %collective-permute-done = bf16[1,512,1024]{2,1,0:T(8,128)(2,1)S(1)} collective-permute-done((bf16[1,512,1024]{2,1,0:T(8,128)(2,1)}, bf16[1,512,1024]{2,1,0:T(8,128)(2,1)S(1)}, u32[]{:S(2)}, u32[]{:S(2)}) %collective-permute-start) | collective-permute-done | bytes 1048608 | tf_op jit(solution)/shard_map/ppermute | solution.py:10
  36.6 8.0 %bitcast_convert_fusion = bf16[2,512,512]{2,0,1:T(2,128)(2,1)} fusion(bf16[1,1,512,2,512]{4,3,0,2,1:T(2,128)(2,1)S(1)} %stack.209, bf16[1,1,512,2,512]{4,3,0,2,1:T(2,128)(2,1)S(1)} %stack.208, bf16[1,1,512,2,512]{4,3,0,2,1:T(2,128)(2,1)} %stack.207, pred[3,2,2]{2,0,1:T(4,128)(4,1)S(1)} %fusion.122), kind=kOutput, calls=%fused_computation.148 | convolution fusion | flops 16252928 | bytes 4194316 | tf_op jit(solution)/shard_map/ksnm,ksimj->snij/dot_general | solution.py:72
  44.6 3.9 convolution_convert_fusion
  49.3 60.3 %all_to_all.23 = bf16[64,1,16,512]{3,2,1,0:T(8,128)(2,1)S(1)} all-to-all(bf16[64,1,16,512]{3,2,1,0:T(8,128)(2,1)S(1)} %constant_dynamic-update-slice_fusion), channel_id=1, replica_groups=mesh['sec'=8,'xy'=64] {'xy'}, dimensions={0} | all-to-all | bytes 2097152 | tf_op jit(solution)/shard_map/all_to_all | solution.py:85
  109.6 25.1 %copy.77 = bf16[1,16,32768]{1,0,2:T(2,128)(2,1)} copy(bf16[1,16,32768]{2,1,0:T(8,128)(2,1)S(1)} %bitcast.422) | data formatting | bytes 2097152 | tf_op jit(solution)/shard_map/reshape | solution.py:84
  135.2 179.2 %reduce = bf16[32768,16]{1,0:T(8,128)(2,1)} reduce(bf16[32768,1,16]{2,1,0:T(2,128)(2,1)} %bitcast.418, bf16[]{:T(256)} %broadcast.323), dimensions={1}, to_apply=%bitcast.414.reduce_sub_computation | reduce | bytes 2097154
  314.4 10.4 %reshape.325 = bf16[8,2,32768]{2,1,0:T(2,128)(2,1)S(1)} reshape(bf16[32768,16]{1,0:T(8,128)(2,1)} %reduce) | data formatting | bytes 2097152
  324.8 25.3 %all_to_all.24 = bf16[8,2,32768]{2,1,0:T(2,128)(2,1)S(1)} all-to-all(bf16[8,2,32768]{2,1,0:T(2,128)(2,1)S(1)} %reshape.325), channel_id=1, replica_groups=mesh['sec'=8,'xy'=64] {'sec'}, dimensions={0} | all-to-all | bytes 2097152 | tf_op jit(solution)/shard_map/all_to_all | solution.py:93
  350.1 12.3 %reshape.326 = bf16[32768,1,16]{2,1,0:T(2,128)(2,1)} reshape(bf16[8,2,32768]{2,1,0:T(2,128)(2,1)S(1)} %all_to_all.24) | data formatting | bytes 2097152
  362.4 29.6 %copy.78 = bf16[1,16,32768]{2,1,0:T(8,128)(2,1)S(1)} copy(bf16[1,16,32768]{1,0,2:T(2,128)(2,1)} %bitcast.419) | data formatting | bytes 2097152 | tf_op jit(solution)/shard_map/all_to_all | solution.py:93
  392.8 3.1 collective-permute-start.2
  398.6 2.6 collective-permute-done.3
  402.7 3.0 collective-permute-start.4
  405.8 4.6 collective-permute-start.5
  412.9 27.6 %fusion.43 = bf16[8,16,4096]{2,0,1:T(8,128)(2,1)} fusion(f32[8,18,4098]{2,0,1:T(8,128)S(1)} %maximum_convert_fusion, f32[]{:T(128)} %bitcast.105, f32[]{:T(128)} %bitcast.104, f32[]{:T(128)} %bitcast.103, f32[]{:T(128)} %bitcast.102, f32[]{:T(128)} %bitcast.101, f32[]{:T(128)} %bitcast.100, f32[]{:T(128)} %bitcast.99, f32[]{:T(128)} %bitcast.98, ...), kind=kLoop, calls=%fused_computation.80 | loop fusion | flops 28835840 | bytes 22356076 | tf_op jit(solution)/shard_map/convert_element_type | solution.py:107
  441.4 3.0 collective-permute-start.6
  447.1 2.6 collective-permute-done.7
  449.7 2.9 concatenate.15
  452.6 2.3 collective-permute-start.8
  454.9 5.7 %collective-permute-start.9 = (bf16[8,1,4098]{2,0,1:T(8,128)(2,1)S(1)}, bf16[8,1,4098]{2,0,1:T(8,128)(2,1)S(1)}, u32[]{:S(2)}, u32[]{:S(2)}) collective-permute-start(bf16[8,1,4098]{2,0,1:T(8,128)(2,1)S(1)} %get-tuple-element.6), channel_id=1, source_target_pairs={{1,0},{2,1},{3,2},{4,3},{5,4},{6,5},{7,6},{8,7},{9,8},{10,9},{11,1... | collective-permute-start | bytes 196712 | tf_op jit(solution)/shard_map/ppermute | solution.py:21
  463.4 27.7 %fusion.89 = bf16[8,16,4096]{2,0,1:T(8,128)(2,1)} fusion(f32[8,18,4098]{2,0,1:T(8,128)S(1)} %maximum_convert_fusion.1, f32[]{:T(128)} %bitcast.131, f32[]{:T(128)} %bitcast.130, f32[]{:T(128)} %bitcast.129, f32[]{:T(128)} %bitcast.128, f32[]{:T(128)} %bitcast.127, f32[]{:T(128)} %bitcast.126, f32[]{:T(128)} %bitcast.125, f32[]{:T(128)} %bitcast.124, ...), kind=kLoop, calls=%fused_computation.126 | loop fusion | flops 29360128 | bytes 23404652 | tf_op jit(solution)/shard_map/convert_element_type | solution.py:112
  491.1 2.8 copy.79
  (115 shorter events, 20.8 us)
Async XLA Ops:
  0.0 16.8 %copy-start.8 = (s32[1,2,2]{2,1,0:T(2,128)S(1)}, s32[1,2,2]{2,1,0:T(2,128)}, u32[]{:S(2)}) copy-start(s32[1,2,2]{2,1,0:T(2,128)} %param.6) | copy-start | bytes 52
  0.0 16.9 %copy-start.7 = (f32[1,2,2]{2,1,0:T(2,128)S(1)}, f32[1,2,2]{2,1,0:T(2,128)}, u32[]{:S(2)}) copy-start(f32[1,2,2]{2,1,0:T(2,128)} %param.7) | copy-start | bytes 52
  0.0 34.2 %collective-permute-start = (bf16[1,512,1024]{2,1,0:T(8,128)(2,1)}, bf16[1,512,1024]{2,1,0:T(8,128)(2,1)S(1)}, u32[]{:S(2)}, u32[]{:S(2)}) collective-permute-start(bf16[1,512,1024]{2,1,0:T(8,128)(2,1)} %param.5), channel_id=1, source_target_pairs={{0,1},{1,2},{2,3},{3,4},{4,5},{5,6},{6,7},{7,8},{8,9},{9,10},{10,1... | collective-permute-start | bytes 3145736 | tf_op jit(solution)/shard_map/ppermute | solution.py:10
  3.7 32.1 %collective-permute-start.1 = (bf16[1,512,1024]{2,1,0:T(8,128)(2,1)}, bf16[1,512,1024]{2,1,0:T(8,128)(2,1)S(1)}, u32[]{:S(2)}, u32[]{:S(2)}) collective-permute-start(bf16[1,512,1024]{2,1,0:T(8,128)(2,1)} %param.5), channel_id=1, source_target_pairs={{1,0},{2,1},{3,2},{4,3},{5,4},{6,5},{7,6},{8,7},{9,8},{10,9},{11,1... | collective-permute-start | bytes 3145736 | tf_op jit(solution)/shard_map/ppermute | solution.py:10
  36.6 8.0 %copy-start.2 = (pred[512,512]{1,0:T(8,128)(4,1)S(1)}, pred[512,512]{1,0:T(8,128)(4,1)}, u32[]{:S(2)}) copy-start(pred[512,512]{1,0:T(8,128)(4,1)} %get-tuple-element.78) | copy-start | bytes 786436
  36.6 8.0 %copy-start.3 = (pred[512,512]{1,0:T(8,128)(4,1)S(1)}, pred[512,512]{1,0:T(8,128)(4,1)}, u32[]{:S(2)}) copy-start(pred[512,512]{1,0:T(8,128)(4,1)} %get-tuple-element.79) | copy-start | bytes 786436
  36.6 8.0 %copy-start.4 = (pred[512,512]{1,0:T(8,128)(4,1)S(1)}, pred[512,512]{1,0:T(8,128)(4,1)}, u32[]{:S(2)}) copy-start(pred[512,512]{1,0:T(8,128)(4,1)} %get-tuple-element.80) | copy-start | bytes 786436
  392.0 5.8 %copy-start.5 = (f32[3,3,3]{2,1,0:T(4,128)S(1)}, f32[3,3,3]{2,1,0:T(4,128)}, u32[]{:S(2)}) copy-start(f32[3,3,3]{2,1,0:T(4,128)} %param.8) | copy-start | bytes 328
  392.8 5.8 %collective-permute-start.2 = (bf16[8,16,1]{2,0,1:T(8,128)(2,1)S(1)}, bf16[8,16,1]{2,0,1:T(8,128)(2,1)S(1)}, u32[]{:S(2)}, u32[]{:S(2)}) collective-permute-start(bf16[8,16,1]{2,0,1:T(8,128)(2,1)S(1)} %get-tuple-element.12), channel_id=1, source_target_pairs={{0,64},{64,128},{128,192},{192,256},{256,320},{320,384},{384,448},... | collective-permute-start | bytes 776 | tf_op jit(solution)/shard_map/ppermute | solution.py:20
  395.9 5.2 %collective-permute-start.3 = (bf16[8,16,1]{2,0,1:T(8,128)(2,1)S(1)}, bf16[8,16,1]{2,0,1:T(8,128)(2,1)S(1)}, u32[]{:S(2)}, u32[]{:S(2)}) collective-permute-start(bf16[8,16,1]{2,0,1:T(8,128)(2,1)S(1)} %get-tuple-element.11), channel_id=1, source_target_pairs={{64,0},{128,64},{192,128},{256,192},{320,256},{384,320},{448,384},... | collective-permute-start | bytes 776 | tf_op jit(solution)/shard_map/ppermute | solution.py:21
  402.7 8.3 %copy-start = (bf16[8,16,4098]{2,0,1:T(8,128)(2,1)}, bf16[8,16,4098]{2,0,1:T(8,128)(2,1)S(1)}, u32[]{:S(2)}) copy-start(bf16[8,16,4098]{2,0,1:T(8,128)(2,1)S(1)} %concatenate.13) | copy-start | bytes 3147268
  402.7 8.3 %collective-permute-start.4 = (bf16[8,1,4098]{2,0,1:T(8,128)(2,1)S(1)}, bf16[8,1,4098]{2,0,1:T(8,128)(2,1)S(1)}, u32[]{:S(2)}, u32[]{:S(2)}) collective-permute-start(bf16[8,1,4098]{2,0,1:T(8,128)(2,1)S(1)} %get-tuple-element.7), channel_id=1, source_target_pairs={{0,1},{1,2},{2,3},{3,4},{4,5},{5,6},{6,7},{7,8},{8,9},{9,10},{10,1... | collective-permute-start | bytes 196712 | tf_op jit(solution)/shard_map/ppermute | solution.py:20
  405.8 5.7 %collective-permute-start.5 = (bf16[8,1,4098]{2,0,1:T(8,128)(2,1)S(1)}, bf16[8,1,4098]{2,0,1:T(8,128)(2,1)S(1)}, u32[]{:S(2)}, u32[]{:S(2)}) collective-permute-start(bf16[8,1,4098]{2,0,1:T(8,128)(2,1)S(1)} %get-tuple-element.8), channel_id=1, source_target_pairs={{1,0},{2,1},{3,2},{4,3},{5,4},{6,5},{7,6},{8,7},{9,8},{10,9},{11,1... | collective-permute-start | bytes 196712 | tf_op jit(solution)/shard_map/ppermute | solution.py:21
  412.9 33.5 %copy-start.6 = (f32[3,3,3]{2,1,0:T(4,128)S(1)}, f32[3,3,3]{2,1,0:T(4,128)}, u32[]{:S(2)}) copy-start(f32[3,3,3]{2,1,0:T(4,128)} %param.9) | copy-start | bytes 328
  441.4 5.7 %collective-permute-start.6 = (bf16[8,16,1]{2,0,1:T(8,128)(2,1)S(1)}, bf16[8,16,1]{2,0,1:T(8,128)(2,1)S(1)}, u32[]{:S(2)}, u32[]{:S(2)}) collective-permute-start(bf16[8,16,1]{2,0,1:T(8,128)(2,1)S(1)} %get-tuple-element.10), channel_id=1, source_target_pairs={{0,64},{64,128},{128,192},{192,256},{256,320},{320,384},{384,448},... | collective-permute-start | bytes 776 | tf_op jit(solution)/shard_map/ppermute | solution.py:20
  444.5 5.2 %collective-permute-start.7 = (bf16[8,16,1]{2,0,1:T(8,128)(2,1)S(1)}, bf16[8,16,1]{2,0,1:T(8,128)(2,1)S(1)}, u32[]{:S(2)}, u32[]{:S(2)}) collective-permute-start(bf16[8,16,1]{2,0,1:T(8,128)(2,1)S(1)} %get-tuple-element.9), channel_id=1, source_target_pairs={{64,0},{128,64},{192,128},{256,192},{320,256},{384,320},{448,384},... | collective-permute-start | bytes 776 | tf_op jit(solution)/shard_map/ppermute | solution.py:21
  452.6 8.7 %copy-start.1 = (bf16[8,16,4098]{2,0,1:T(8,128)(2,1)}, bf16[8,16,4098]{2,0,1:T(8,128)(2,1)S(1)}, u32[]{:S(2)}) copy-start(bf16[8,16,4098]{2,0,1:T(8,128)(2,1)S(1)} %concatenate.15) | copy-start | bytes 3147268
  452.6 8.7 %collective-permute-start.8 = (bf16[8,1,4098]{2,0,1:T(8,128)(2,1)S(1)}, bf16[8,1,4098]{2,0,1:T(8,128)(2,1)S(1)}, u32[]{:S(2)}, u32[]{:S(2)}) collective-permute-start(bf16[8,1,4098]{2,0,1:T(8,128)(2,1)S(1)} %get-tuple-element.5), channel_id=1, source_target_pairs={{0,1},{1,2},{2,3},{3,4},{4,5},{5,6},{6,7},{7,8},{8,9},{9,10},{10,1... | collective-permute-start | bytes 196712 | tf_op jit(solution)/shard_map/ppermute | solution.py:20
  454.9 7.0 %collective-permute-start.9 = (bf16[8,1,4098]{2,0,1:T(8,128)(2,1)S(1)}, bf16[8,1,4098]{2,0,1:T(8,128)(2,1)S(1)}, u32[]{:S(2)}, u32[]{:S(2)}) collective-permute-start(bf16[8,1,4098]{2,0,1:T(8,128)(2,1)S(1)} %get-tuple-element.6), channel_id=1, source_target_pairs={{1,0},{2,1},{3,2},{4,3},{5,4},{6,5},{7,6},{8,7},{9,8},{10,9},{11,1... | collective-permute-start | bytes 196712 | tf_op jit(solution)/shard_map/ppermute | solution.py:21
